TPU v7x, 256 devices: a whole 4x4x8 slice. The times are simulated.
256 devices in a mesh: pipe: 2 (over core), slab: 8 (over x, z_hi), dp: 16 (over z_lo, y).
Axes of the slice: x: 4, y: 4, z: 8 (z_hi: 2, z_lo: 4; z = z_hi * 4 + z_lo), core: 2. Of those that a mesh axis runs over, the one named last changes fastest.
Arguments:
- saved_inputs: bfloat16 [2, 2, 16, 2, 16, 16, 512], P('pipe', None, 'dp', None, 'slab'), may hold values from -12 to 12
- loss_cotangent: bfloat16 [2, 16, 2, 16, 16, 512], P(None, 'dp', None, 'slab'), may hold values from -3 to 3
- upstream: bfloat16 [16, 2, 16, 16, 512], P('dp', None, 'slab'), may hold values from -3 to 3
- conv_weight: bfloat16 [2, 512, 13824], P('pipe', 'dp'), may hold values from -0.0546875 to 0.0546875
- adagn_table: bfloat16 [2, 1000, 1024], P('pipe'), may hold values from -3 to 3
- timesteps: int32 [3, 16], P(None, 'dp'), may hold values from 0 to 999
- frame_counts: int32 [3, 16], P(None, 'dp'), may hold values from 1 to 2
Outputs:
- input_grads: bfloat16 [2, 2, 16, 2, 16, 16, 512], P('pipe', None, 'dp', None, 'slab')
- weight_grad: float32 [2, 512, 13824], P('pipe', 'dp')
- embed_grad: float32 [2, 2, 16, 1024], P('pipe', None, 'dp')
All inputs are finite; a program needn't handle non-finite values.
Results may differ from a plain program's by a relative error of at most 0.015.
Values may be sent and summed in bfloat16 or wider, within the bound.
A program may use at most 128 MiB of HBM per device.

v0:
```python
import math
import jax
import jax.numpy as jnp
from jax import lax
from jax.sharding import PartitionSpec as P

GROUPS = 32
EPS = 1e-05


def extended(x, sides, width):
    for axis, dim in sides:
        devices, length = (lax.axis_size(axis), x.shape[dim])
        up = [(i, (i + 1) % devices) for i in range(devices - 1)]
        down = [(j, i) for i, j in up]
        last = lax.slice_in_dim(x, length - width, length, axis=dim)
        initial = lax.slice_in_dim(x, 0, width, axis=dim)
        before = lax.ppermute(last, axis, up)
        after = lax.ppermute(initial, axis, down)
        x = jnp.concatenate([before, x, after], axis=dim)
    return x


def shifted(block, axis, distance):
    devices = range(lax.axis_size(axis))
    route = [(i - distance, i) for i in devices if i - distance in devices]
    return lax.ppermute(block, axis, route)


def group_sums(values, groups):
    summed = jnp.sum(values.reshape(-1, values.shape[-1]), axis=0)
    return jnp.sum(summed.reshape(groups, -1), axis=1)


def silu_grad(preact):
    sigma = jax.nn.sigmoid(preact)
    return sigma * (1.0 + preact * (1.0 - sigma))


def hidden_of(values, mean_c, rstd_c, gain_row, bias_row, mask_now):
    normed = (values - mean_c) * rstd_c
    preact = normed * gain_row + bias_row
    activated = jax.nn.silu(preact) * mask_now[:, None, None, None]
    return (normed, preact, activated)


def norm_terms(moment_one, moment_two, count_now):
    mean_g = moment_one / count_now
    var_g = moment_two / count_now - mean_g * mean_g
    return (mean_g, lax.rsqrt(var_g + EPS))


def tap_stack(padded, frames, slab_rows, cells_wide, mirrored):
    slices = []
    for depth_at in range(3):
        for vertical in range(3):
            for across in range(3):
                if mirrored:
                    offsets = (2 - depth_at, 2 - vertical, 2 - across)
                else:
                    offsets = (depth_at, vertical, across)
                slices.append(
                    padded[
                        ...,
                        offsets[0] : offsets[0] + frames,
                        offsets[1] : offsets[1] + slab_rows,
                        offsets[2] : offsets[2] + cells_wide,
                        :,
                    ]
                )
    return jnp.stack(slices, 0)


def pad_cells(values):
    return jnp.pad(values, ((1, 1), (0, 0), (1, 1), (0, 0)))


def local(
    saved_inputs, loss_cotangent, upstream, conv_weight, adagn_table, timesteps, frame_counts
):
    section_index = lax.axis_index("pipe")
    slab_count = lax.axis_size("slab")
    replicas = lax.axis_size("dp")
    inputs = saved_inputs[0, :, 0]
    tick_count, frames, slab_rows, cells_wide, channels = inputs.shape
    groups = GROUPS
    per_group = channels // groups
    height_total = slab_rows * slab_count
    step_table = adagn_table[0]
    weight_local = conv_weight[0]
    steps_now = lax.dynamic_slice_in_dim(timesteps[:, 0], section_index, tick_count)
    counts_now = lax.dynamic_slice_in_dim(frame_counts[:, 0], section_index, tick_count)
    onehot = (
        steps_now[:, None] == jnp.arange(step_table.shape[0], dtype=jnp.int32)[None, :]
    ).astype(jnp.bfloat16)
    embedded = jnp.dot(onehot, step_table, preferred_element_type=jnp.float32)
    scales = 1.0 + embedded[:, :channels]
    shifts = embedded[:, channels:]
    frame_masks = (jnp.arange(frames, dtype=jnp.int32)[None, :] < counts_now[:, None]).astype(
        jnp.float32
    )
    valid_counts = counts_now.astype(jnp.float32) * float(height_total * cells_wide * per_group)
    weight_norm = 1.0 / math.sqrt(tick_count * replicas * frames * height_total * cells_wide)
    embed_norm = 1.0 / math.sqrt(frames * height_total * cells_wide)
    full_weight = lax.all_gather(weight_local, "dp", axis=0, tiled=True).reshape(
        channels, 27, channels
    )
    dx_list = []
    embed_list = []
    hidden_exts = []
    cotangents = []
    received = None
    for tick_index in range(tick_count):
        values = inputs[tick_index].astype(jnp.float32)
        masked = values * frame_masks[tick_index][:, None, None, None]
        part_one = group_sums(masked, groups)
        part_two = group_sums(masked * values, groups)
        moment_one, moment_two = lax.psum((part_one, part_two), "slab")
        count_now = valid_counts[tick_index]
        mean_g, rstd_g = norm_terms(moment_one, moment_two, count_now)
        mean_c = jnp.repeat(mean_g, per_group)
        rstd_c = jnp.repeat(rstd_g, per_group)
        mask_now = frame_masks[tick_index]
        normed, preact, activated = hidden_of(
            inputs[tick_index].astype(jnp.float32),
            mean_c,
            rstd_c,
            scales[tick_index],
            shifts[tick_index],
            mask_now,
        )
        hidden_ext = extended(activated.astype(jnp.bfloat16), (("slab", 1),), 1)
        hidden_exts.append(hidden_ext)
        incoming = upstream[0] if tick_index == 0 else received
        cotangent = jnp.where(section_index == 1, loss_cotangent[tick_index, 0], incoming)
        cot_rows = extended(cotangent, (("slab", 1),), 1)
        cot_pad = pad_cells(cot_rows)
        tap_slices = tap_stack(cot_pad, frames, slab_rows, cells_wide, True)
        upward = jnp.einsum(
            "tfrwo,oti->frwi", tap_slices, full_weight, preferred_element_type=jnp.float32
        )
        pre_grad = upward * silu_grad(preact) * mask_now[:, None, None, None]
        dnormed = pre_grad * scales[tick_index]
        part_a = group_sums(dnormed, groups)
        part_b = group_sums(dnormed * normed, groups)
        scale_part = jnp.sum(pre_grad * normed, axis=(0, 1, 2))
        shift_part = jnp.sum(pre_grad, axis=(0, 1, 2))
        sum_a, sum_b, scale_sum, shift_sum = lax.psum(
            (part_a, part_b, scale_part, shift_part), "slab"
        )
        branch = (
            rstd_c
            * (
                dnormed
                - jnp.repeat(sum_a / count_now, per_group)
                - normed * jnp.repeat(sum_b / count_now, per_group)
            )
            * mask_now[:, None, None, None]
        )
        result = (cotangent.astype(jnp.float32) + branch).astype(jnp.bfloat16)
        dx_list.append(result)
        embed_list.append(jnp.concatenate([scale_sum, shift_sum]) * embed_norm)
        cotangents.append(cotangent)
        if tick_index + 1 < tick_count:
            received = shifted(result, "pipe", -1)
    cot_all = jnp.stack(cotangents)
    shard_rows = weight_local.shape[0]
    hidden_all = jnp.stack([pad_cells(one_ext) for one_ext in hidden_exts])
    hidden_taps = tap_stack(hidden_all, frames, slab_rows, cells_wide, False)
    grad_term = jnp.einsum(
        "kfrwo,tkfrwi->oti", cot_all, hidden_taps, preferred_element_type=jnp.float32
    )
    grad_shard = lax.psum_scatter(
        (grad_term.reshape(lax.axis_size("dp") * shard_rows, -1) * weight_norm).astype(
            jnp.bfloat16
        ),
        "dp",
        scatter_dimension=0,
        tiled=True,
    ).astype(jnp.float32)
    weight_grad = lax.psum(grad_shard, "slab")
    input_grads = jnp.stack(dx_list)[None, :, None]
    embed_grad = jnp.stack(embed_list)[None, :, None]
    return (input_grads, weight_grad[None], embed_grad)


def solution(mesh):
    placed = (
        P("pipe", None, "dp", None, "slab", None, None),
        P(None, "dp", None, "slab", None, None),
        P("dp", None, "slab", None, None),
        P("pipe", "dp", None),
        P("pipe", None, None),
        P(None, "dp"),
        P(None, "dp"),
    )
    return jax.shard_map(
        local,
        mesh=mesh,
        in_specs=placed,
        out_specs=(
            P("pipe", None, "dp", None, "slab", None, None),
            P("pipe", "dp", None),
            P("pipe", None, "dp", None),
        ),
        check_vma=False,
    )
```

profile of v0, /device:TPU:8, one launch (start us, length us, event | category | flops | bytes accessed | tf_op | source)
XLA Modules:
  0.0 686.2 jit_solution(7426702432679894269)
XLA Ops:
  7.2 0.7 all-gather.3.cloned.1.call-update
  8.0 0.9 bitcast_select_fusion.2
  8.9 9.1 %collective-permute-start = (bf16[2,1,16,512]{3,2,1,0:T(8,128)(2,1)S(1)}, bf16[2,1,16,512]{3,2,1,0:T(8,128)(2,1)S(1)}, u32[]{:S(2)}, u32[]{:S(2)}) collective-permute-start(bf16[2,1,16,512]{3,2,1,0:T(8,128)(2,1)S(1)} %get-tuple-element.56), channel_id=1, source_target_pairs={{0,16},{16,32},{32,48},{48,64},{64,80},{80,96},{96,112},{1,17},{17... | collective-permute-start | bytes 98312 | tf_op jit(solution)/shard_map/ppermute | solution.py:18
  18.0 1.3 collective-permute-start.1
  19.3 0.7 convert_multiply_fusion.4
  20.1 1.0 fusion.43
  21.5 32.6 %all-reduce.6 = (f32[32]{0:T(128)S(1)}, f32[32]{0:T(128)S(1)}) all-reduce(f32[32]{0:T(128)S(1)} %reduce_sum.183, f32[32]{0:T(128)S(1)} %reduce_sum.181), channel_id=1, replica_groups=mesh['pipe'=2,'slab'=8,'dp'=16] {'slab'}, use_global_device_ids=true, to_apply=%region_5.0 | all-reduce | flops 64 | bytes 512 | tf_op jit(solution)/shard_map/psum | solution.py:118
  54.1 0.7 dynamic-slice_bitcast_fusion
  55.9 0.7 add_rsqrt_fusion.1
  57.3 0.7 constant_dynamic-update-slice_fusion.26
  58.0 0.6 constant_dynamic-update-slice_fusion.25
  58.6 0.6 constant_dynamic-update-slice_fusion.24
  59.3 0.6 constant_dynamic-update-slice_fusion.23
  59.9 0.6 constant_dynamic-update-slice_fusion.22
  60.6 0.6 constant_dynamic-update-slice_fusion.21
  61.2 0.6 constant_dynamic-update-slice_fusion.20
  61.9 0.6 constant_dynamic-update-slice_fusion.19
  62.5 0.6 constant_dynamic-update-slice_fusion.18
  63.1 0.6 constant_dynamic-update-slice_fusion.17
  63.8 0.6 constant_dynamic-update-slice_fusion.16
  64.4 0.6 constant_dynamic-update-slice_fusion.15
  65.1 0.6 constant_dynamic-update-slice_fusion.14
  65.7 0.6 constant_dynamic-update-slice_fusion.13
  66.4 0.6 constant_dynamic-update-slice_fusion.12
  67.0 0.6 constant_dynamic-update-slice_fusion.11
  67.7 0.6 constant_dynamic-update-slice_fusion.10
  68.3 0.6 constant_dynamic-update-slice_fusion.9
  68.9 0.6 constant_dynamic-update-slice_fusion.8
  69.6 0.6 constant_dynamic-update-slice_fusion.7
  70.2 0.6 constant_dynamic-update-slice_fusion.6
  70.9 0.6 constant_dynamic-update-slice_fusion.5
  71.5 0.6 constant_dynamic-update-slice_fusion.4
  72.2 0.6 constant_dynamic-update-slice_fusion.3
  72.8 0.6 constant_dynamic-update-slice_fusion.2
  73.4 0.6 constant_dynamic-update-slice_fusion.1
  74.1 0.6 constant_dynamic-update-slice_fusion
  74.7 94.1 %all-gather.3.cloned.1.call-done = bf16[1,512,13824]{2,1,0:T(8,128)(2,1)} async-done(((bf16[1,32,13824]{2,1,0:T(8,128)(2,1)}), bf16[1,512,13824]{2,1,0:T(8,128)(2,1)}) %all-gather.3.cloned.1.call-update) | async-done | bytes 14155792 | tf_op jit(solution)/shard_map/all_gather | solution.py:105
  168.8 18.7 %copy.101 = bf16[1,512,13824]{1,2,0:T(8,128)(2,1)} copy(bf16[1,512,13824]{2,1,0:T(8,128)(2,1)} %all-gather.3.cloned.1.call-done) | data formatting | bytes 28311552 | tf_op jit(solution)/shard_map/all_gather | solution.py:105
  187.5 10.0 %fusion.42 = (f32[512]{0:T(512)S(1)}, f32[512]{0:T(512)S(1)}, f32[512]{0:T(512)S(1)}, f32[512]{0:T(512)S(1)}, f32[2,2,16,512]{3,2,1,0:T(8,128)S(1)}) fusion(f32[512]{0:T(512)S(1)} %sub.59, f32[512]{0:T(512)S(1)} %mul.241, bf16[1,2,1,2,2,16,512]{6,5,4,3,2,1,0:T(8,128)(2,1)S(1)} %copy-done.3, f32[512]{0:T(512)S(1)} %bitcast.570, ...), kind=kOutput, calls=%fused_computation.194 | convolution fusion | flops 906655744 | bytes 16138248 | tf_op jit(solution)/shard_map/tfrwo,oti->frwi/dot_general | solution.py:139
  197.9 31.7 %all-reduce.5 = (f32[32]{0:T(128)S(1)}, f32[32]{0:T(128)S(1)}, f32[32]{0:T(128)S(1)}, f32[32]{0:T(128)S(1)}) all-reduce(f32[32]{0:T(128)S(1)} %reduce_sum.187, f32[32]{0:T(128)S(1)} %reduce_sum.185, f32[32]{0:T(128)S(1)} %reduce_sum.191, f32[32]{0:T(128)S(1)} %reduce_sum.189), channel_id=1, replica_groups=mesh['pipe'=2,'slab'=8,'dp'=16] {'slab'}, use_global_device_ids=true, to_apply=%region_11.12 | all-reduce | flops 128 | bytes 1024 | tf_op jit(solution)/shard_map/psum | solution.py:148
  229.6 0.6 broadcast_divide_fusion.3
  230.7 1.3 collective-permute-start.2
  232.0 1.8 collective-permute-done.2
  233.8 1.3 collective-permute-start.3
  235.1 1.3 collective-permute-start.4
  236.4 0.7 add_rsqrt_fusion
  237.4 8.5 %collective-permute-start.5 = (bf16[2,1,16,512]{3,2,1,0:T(8,128)(2,1)S(1)}, bf16[2,1,16,512]{3,2,1,0:T(8,128)(2,1)S(1)}, u32[]{:S(2)}, u32[]{:S(2)}) collective-permute-start(bf16[2,1,16,512]{3,2,1,0:T(8,128)(2,1)S(1)} %get-tuple-element.52), channel_id=1, source_target_pairs={{0,16},{16,32},{32,48},{48,64},{64,80},{80,96},{96,112},{1,17},{17... | collective-permute-start | bytes 98312 | tf_op jit(solution)/shard_map/ppermute | solution.py:18
  245.9 1.3 collective-permute-start.6
  247.9 9.4 %fusion.6 = f32[2,2,16,512]{3,2,0,1:T(8,128)S(1)} fusion(bf16[512,27,512,1,1]{0,2,3,4,1:T(8,128)(2,1)} %bitcast.562, bf16[27,2,2,16,512]{4,3,2,1,0:T(8,128)(2,1)S(1)} %constant_dynamic-update-slice_fusion.27), kind=kOutput, calls=%fused_computation.63 | convolution fusion | flops 905969664 | bytes 16056320 | tf_op jit(solution)/shard_map/tfrwo,oti->frwi/dot_general | solution.py:139
  257.5 8.7 %collective-permute-start.7 = (bf16[2,1,16,512]{3,2,1,0:T(8,128)(2,1)S(1)}, bf16[2,1,16,512]{3,2,1,0:T(8,128)(2,1)S(1)}, u32[]{:S(2)}, u32[]{:S(2)}) collective-permute-start(bf16[2,1,16,512]{3,2,1,0:T(8,128)(2,1)S(1)} %get-tuple-element.50), channel_id=1, source_target_pairs={{0,16},{16,32},{32,48},{48,64},{64,80},{80,96},{96,112},{1,17},{17... | collective-permute-start | bytes 98312 | tf_op jit(solution)/shard_map/ppermute | solution.py:18
  266.2 1.3 collective-permute-start.8
  267.8 9.0 %collective-permute-done.8 = bf16[2,1,16,512]{3,2,1,0:T(8,128)(2,1)S(1)} collective-permute-done((bf16[2,1,16,512]{3,2,1,0:T(8,128)(2,1)S(1)}, bf16[2,1,16,512]{3,2,1,0:T(8,128)(2,1)S(1)}, u32[]{:S(2)}, u32[]{:S(2)}) %collective-permute-start.8) | collective-permute-done | bytes 32800 | tf_op jit(solution)/shard_map/ppermute | solution.py:19
  278.0 1.7 copy-done.2
  279.7 9.1 %fusion = bf16[512,27,512]{0,2,1:T(8,128)(2,1)} fusion(bf16[27,2,2,2,16,512]{5,4,3,2,1,0:T(8,128)(2,1)} %copy-done.2, bf16[1,2,2,16,512]{4,3,2,1,0:T(8,128)(2,1)S(1)} %bitcast.564, bf16[1,2,2,16,512]{4,3,2,1,0:T(8,128)(2,1)S(1)} %get-tuple-element.46), kind=kOutput, calls=%fused_computation.1 | convolution fusion | flops 1826160640 | bytes 17825792 | tf_op jit(solution)/shard_map/kfrwo,tkfrwi->oti/dot_general | solution.py:170
  288.8 18.6 %copy.108 = bf16[512,13824]{1,0:T(8,128)(2,1)} copy(bf16[512,13824]{0,1:T(8,128)(2,1)} %bitcast.563) | data formatting | bytes 28311552 | tf_op jit(solution)/shard_map/convert_element_type | solution.py:174
  307.5 193.0 %reduce-scatter.2.cloned.1.call-done = bf16[32,13824]{1,0:T(8,128)(2,1)} async-done(((bf16[512,13824]{1,0:T(8,128)(2,1)}), bf16[32,13824]{1,0:T(8,128)(2,1)}) %reduce-scatter.2.cloned.1.call-update) | async-done | bytes 884752 | tf_op jit(solution)/shard_map/reduce_scatter | solution.py:173
  500.5 2.5 bitcast_convert_fusion
  503.5 35.7 %all-reduce.4 = (f32[32]{0:T(128)S(1)}, f32[32]{0:T(128)S(1)}, f32[1,512]{1,0:T(1,128)S(1)}, f32[1,512]{1,0:T(1,128)S(1)}, f32[1,512]{1,0:T(1,128)S(1)}, /*index=5*/f32[1,512]{1,0:T(1,128)S(1)}) all-reduce(f32[32]{0:T(128)S(1)} %reduce_sum.195, f32[32]{0:T(128)S(1)} %reduce_sum.193, ...), channel_id=1, replica_groups=mesh['pipe'=2,'slab'=8,'dp'=16] {'slab'}, use_global_device_ids=true, to_apply=%region_23.24 | all-reduce | flops 2112 | bytes 16896 | tf_op jit(solution)/shard_map/psum | solution.py:148
  539.2 0.6 broadcast_in_dim.47
  539.8 0.6 broadcast_divide_fusion.1
  540.6 0.7 broadcast_divide_fusion
  541.5 0.7 maximum_bitcast_fusion
  542.2 134.7 %all-reduce.9.cloned.1.call-done = f32[1,32,13824]{2,1,0:T(8,128)} async-done(((f32[1,32,13824]{2,1,0:T(8,128)}), f32[1,32,13824]{2,1,0:T(8,128)}) %all-reduce.9.cloned.1.call-update) | async-done | bytes 1769488 | tf_op jit(solution)/shard_map/psum | solution.py:181
  676.9 2.8 copy.209
  (131 shorter events, 6.2 us)
Async XLA Ops:
  7.2 48.2 %copy-start = (bf16[1,1000,1024]{2,1,0:T(8,128)(2,1)S(1)}, bf16[1,1000,1024]{2,1,0:T(8,128)(2,1)}, u32[]{:S(2)}) copy-start(bf16[1,1000,1024]{2,1,0:T(8,128)(2,1)} %param.11) | copy-start | bytes 6144004
  7.2 161.6 %all-gather.3.cloned.1.call-start = ((), (), s32[]{:S(2)}) async-start(), calls=%async_computation.3 | async-start | bytes 15040512 | tf_op jit(solution)/shard_map/all_gather | solution.py:105
  7.9 492.6 %reduce-scatter.2.cloned.1.call-start = ((), (), s32[]{:S(2)}) async-start(), calls=%async_computation.1 | async-start | bytes 15040512 | tf_op jit(solution)/shard_map/reduce_scatter | solution.py:173
  8.9 48.4 %collective-permute-start = (bf16[2,1,16,512]{3,2,1,0:T(8,128)(2,1)S(1)}, bf16[2,1,16,512]{3,2,1,0:T(8,128)(2,1)S(1)}, u32[]{:S(2)}, u32[]{:S(2)}) collective-permute-start(bf16[2,1,16,512]{3,2,1,0:T(8,128)(2,1)S(1)} %get-tuple-element.56), channel_id=1, source_target_pairs={{0,16},{16,32},{32,48},{48,64},{64,80},{80,96},{96,112},{1,17},{17... | collective-permute-start | bytes 98312 | tf_op jit(solution)/shard_map/ppermute | solution.py:18
  18.0 39.3 %collective-permute-start.1 = (bf16[2,1,16,512]{3,2,1,0:T(8,128)(2,1)S(1)}, bf16[2,1,16,512]{3,2,1,0:T(8,128)(2,1)S(1)}, u32[]{:S(2)}, u32[]{:S(2)}) collective-permute-start(bf16[2,1,16,512]{3,2,1,0:T(8,128)(2,1)S(1)} %get-tuple-element.57), channel_id=1, source_target_pairs={{16,0},{32,16},{48,32},{64,48},{80,64},{96,80},{112,96},{17,1},{33... | collective-permute-start | bytes 98312 | tf_op jit(solution)/shard_map/ppermute | solution.py:19
  55.4 10.3 %copy-start.4 = (bf16[2,1,2,2,16,512]{5,4,3,2,1,0:T(8,128)(2,1)S(1)}, bf16[2,1,2,2,16,512]{5,4,3,2,1,0:T(8,128)(2,1)}, u32[]{:S(2)}) copy-start(bf16[2,1,2,2,16,512]{5,4,3,2,1,0:T(8,128)(2,1)} %param.8) | copy-start | bytes 393220
  55.4 10.3 %copy-start.5 = (bf16[1,2,2,16,512]{4,3,2,1,0:T(8,128)(2,1)S(1)}, bf16[1,2,2,16,512]{4,3,2,1,0:T(8,128)(2,1)}, u32[]{:S(2)}) copy-start(bf16[1,2,2,16,512]{4,3,2,1,0:T(8,128)(2,1)} %param.9) | copy-start | bytes 196612
  74.7 112.8 %copy-start.3 = (bf16[1,2,1,2,2,16,512]{6,5,4,3,2,1,0:T(8,128)(2,1)S(1)}, bf16[1,2,1,2,2,16,512]{6,5,4,3,2,1,0:T(8,128)(2,1)}, u32[]{:S(2)}) copy-start(bf16[1,2,1,2,2,16,512]{6,5,4,3,2,1,0:T(8,128)(2,1)} %param.7) | copy-start | bytes 393220
  230.7 3.1 collective-permute-start.2
  233.8 13.3 %collective-permute-start.3 = (bf16[2,1,16,512]{3,2,1,0:T(8,128)(2,1)S(1)}, bf16[2,1,16,512]{3,2,1,0:T(8,128)(2,1)S(1)}, u32[]{:S(2)}, u32[]{:S(2)}) collective-permute-start(bf16[2,1,16,512]{3,2,1,0:T(8,128)(2,1)S(1)} %get-tuple-element.54), channel_id=1, source_target_pairs={{0,16},{16,32},{32,48},{48,64},{64,80},{80,96},{96,112},{1,17},{17... | collective-permute-start | bytes 98312 | tf_op jit(solution)/shard_map/ppermute | solution.py:18
  235.1 12.0 %collective-permute-start.4 = (bf16[2,1,16,512]{3,2,1,0:T(8,128)(2,1)S(1)}, bf16[2,1,16,512]{3,2,1,0:T(8,128)(2,1)S(1)}, u32[]{:S(2)}, u32[]{:S(2)}) collective-permute-start(bf16[2,1,16,512]{3,2,1,0:T(8,128)(2,1)S(1)} %get-tuple-element.55), channel_id=1, source_target_pairs={{16,0},{32,16},{48,32},{64,48},{80,64},{96,80},{112,96},{17,1},{33... | collective-permute-start | bytes 98312 | tf_op jit(solution)/shard_map/ppermute | solution.py:19
  237.4 30.1 %collective-permute-start.5 = (bf16[2,1,16,512]{3,2,1,0:T(8,128)(2,1)S(1)}, bf16[2,1,16,512]{3,2,1,0:T(8,128)(2,1)S(1)}, u32[]{:S(2)}, u32[]{:S(2)}) collective-permute-start(bf16[2,1,16,512]{3,2,1,0:T(8,128)(2,1)S(1)} %get-tuple-element.52), channel_id=1, source_target_pairs={{0,16},{16,32},{32,48},{48,64},{64,80},{80,96},{96,112},{1,17},{17... | collective-permute-start | bytes 98312 | tf_op jit(solution)/shard_map/ppermute | solution.py:18
  245.9 21.6 %collective-permute-start.6 = (bf16[2,1,16,512]{3,2,1,0:T(8,128)(2,1)S(1)}, bf16[2,1,16,512]{3,2,1,0:T(8,128)(2,1)S(1)}, u32[]{:S(2)}, u32[]{:S(2)}) collective-permute-start(bf16[2,1,16,512]{3,2,1,0:T(8,128)(2,1)S(1)} %get-tuple-element.53), channel_id=1, source_target_pairs={{16,0},{32,16},{48,32},{64,48},{80,64},{96,80},{112,96},{17,1},{33... | collective-permute-start | bytes 98312 | tf_op jit(solution)/shard_map/ppermute | solution.py:19
  257.5 10.3 %collective-permute-start.7 = (bf16[2,1,16,512]{3,2,1,0:T(8,128)(2,1)S(1)}, bf16[2,1,16,512]{3,2,1,0:T(8,128)(2,1)S(1)}, u32[]{:S(2)}, u32[]{:S(2)}) collective-permute-start(bf16[2,1,16,512]{3,2,1,0:T(8,128)(2,1)S(1)} %get-tuple-element.50), channel_id=1, source_target_pairs={{0,16},{16,32},{32,48},{48,64},{64,80},{80,96},{96,112},{1,17},{17... | collective-permute-start | bytes 98312 | tf_op jit(solution)/shard_map/ppermute | solution.py:18
  266.2 10.6 %collective-permute-start.8 = (bf16[2,1,16,512]{3,2,1,0:T(8,128)(2,1)S(1)}, bf16[2,1,16,512]{3,2,1,0:T(8,128)(2,1)S(1)}, u32[]{:S(2)}, u32[]{:S(2)}) collective-permute-start(bf16[2,1,16,512]{3,2,1,0:T(8,128)(2,1)S(1)} %get-tuple-element.51), channel_id=1, source_target_pairs={{16,0},{32,16},{48,32},{64,48},{80,64},{96,80},{112,96},{17,1},{33... | collective-permute-start | bytes 98312 | tf_op jit(solution)/shard_map/ppermute | solution.py:19
  278.0 1.7 copy-start.2
  307.5 369.4 %all-reduce.9.cloned.1.call-start = ((), (), s32[]{:S(2)}) async-start(), calls=%async_computation.2 | async-start | bytes 3538944 | tf_op jit(solution)/shard_map/psum | solution.py:181
  541.5 138.2 %copy-start.1 = (bf16[1,1000,1024]{2,1,0:T(8,128)(2,1)S(1)}, bf16[1,1000,1024]{2,1,0:T(8,128)(2,1)}, u32[]{:S(2)}) copy-start(bf16[1,1000,1024]{2,1,0:T(8,128)(2,1)} %param.11) | copy-start | bytes 6144004
Sparse Core Ops, SparseCore 0:
  9.8 158.9 all-gather.2
  307.6 192.8 reduce-scatter.1
  503.8 173.0 all-reduce.8
where the time goes:
time: 688 us; the launch traced here: 686 us
  waiting for transfers between devices  434 us (63%)
  blocking collectives  100 us (15%)
  local copies, waits for them, and re-layouts  61.5 us (9%)
  starting transfers between devices  34.2 us (5%)
  matrix products  28.9 us (4%)
  between operations  14.6 us (2%)
  other arithmetic  13.5 us (2%)
    reduce_scatter x1, waiting for transfers between devices, local(): lax.psum_scatter((grad_term.reshape(lax.axis_size('dp') * shard_rows, -1)...  193 us
    psum x1, waiting for transfers between devices, local(): weight_grad = lax.psum(grad_shard, 'slab')  135 us
    all_gather x1, waiting for transfers between devices, local(): lax.all_gather(weight_local, 'dp', axis=0, tiled=True)  94.1 us
    psum x2, blocking collectives, local(): lax.psum((part_a, part_b, scale_part, shift_part), 'slab')  67.4 us
    psum x1, blocking collectives, local(): moment_one, moment_two = lax.psum((part_one, part_two), 'slab')  32.6 us
    ppermute x4, starting transfers between devices, extended(): before = lax.ppermute(last, axis, up)  27.6 us
    unnamed x60, local copies, waits for them, and re-layouts  19.8 us
    dot_general x2, matrix products, local(): jnp.einsum('tfrwo,oti->frwi', tap_slices, full_weight, preferred_element_...  19.4 us
  transfers between devices with their start and end apart: 12, of which 6 were waited for; matrix products, arithmetic and copies ran while one was open for 6% of the time, Pallas kernels for 0%

commit v1 on v0

--- a/solution.py
+++ b/solution.py
@@ -178,7 +178,7 @@
         scatter_dimension=0,
         tiled=True,
     ).astype(jnp.float32)
-    weight_grad = lax.psum(grad_shard, "slab")
+    weight_grad = jnp.sum(lax.all_gather(grad_shard, "slab"), axis=0)
     input_grads = jnp.stack(dx_list)[None, :, None]
     embed_grad = jnp.stack(embed_list)[None, :, None]
     return (input_grads, weight_grad[None], embed_grad)

time: 688 us -> 787 us (1.14)
  waiting for transfers between devices: 434 us -> 528 us
    all_gather x0 -> x1, waiting for transfers between devices: none -> 229 us  [local(): weight_grad = jnp.sum(lax.all_gather(grad_shard, 'slab'), axis=0)]
    psum x1 -> x0, waiting for transfers between devices: 135 us -> none  [local(): weight_grad = lax.psum(grad_shard, 'slab')]
    unnamed x60 -> x59, local copies, waits for them, and re-layouts: 19.8 us -> 17 us
  transfers between devices with their start and end apart: 12 -> 12, of which waited for: 6 -> 6; matrix products, arithmetic and copies ran while one was open for 6% -> 5% of each run, Pallas kernels for 0% -> 0%
where the time goes in v1:
time: 787 us; the launch traced here: 785 us
  waiting for transfers between devices  528 us (67%)
  blocking collectives  99.5 us (13%)
  local copies, waits for them, and re-layouts  58.7 us (7%)
  starting transfers between devices  34.2 us (4%)
  matrix products  28.9 us (4%)
  other arithmetic  20.8 us (3%)
  between operations  14.5 us (2%)
    all_gather x1, waiting for transfers between devices, local(): weight_grad = jnp.sum(lax.all_gather(grad_shard, 'slab'), axis=0)  229 us
    reduce_scatter x1, waiting for transfers between devices, local(): lax.psum_scatter((grad_term.reshape(lax.axis_size('dp') * shard_rows, -1)...  193 us
    all_gather x1, waiting for transfers between devices, local(): lax.all_gather(weight_local, 'dp', axis=0, tiled=True)  94.1 us
    psum x2, blocking collectives, local(): lax.psum((part_a, part_b, scale_part, shift_part), 'slab')  66.9 us
    psum x1, blocking collectives, local(): moment_one, moment_two = lax.psum((part_one, part_two), 'slab')  32.6 us
    ppermute x4, starting transfers between devices, extended(): before = lax.ppermute(last, axis, up)  27.6 us
    dot_general x2, matrix products, local(): jnp.einsum('tfrwo,oti->frwi', tap_slices, full_weight, preferred_element_...  19.4 us
    all_gather x1, local copies, waits for them, and re-layouts, local(): lax.all_gather(weight_local, 'dp', axis=0, tiled=True)  18.7 us
  transfers between devices with their start and end apart: 12, of which 6 were waited for; matrix products, arithmetic and copies ran while one was open for 5% of the time, Pallas kernels for 0%

profile of v1, /device:TPU:8, one launch (start us, length us, event | category | flops | bytes accessed | tf_op | source)
XLA Modules:
  0.0 785.0 jit_solution(15311315669809999408)
XLA Ops:
  7.2 0.7 all-gather.5.cloned.1.call-update
  8.0 0.9 bitcast_select_fusion.2
  8.9 9.1 %collective-permute-start = (bf16[2,1,16,512]{3,2,1,0:T(8,128)(2,1)S(1)}, bf16[2,1,16,512]{3,2,1,0:T(8,128)(2,1)S(1)}, u32[]{:S(2)}, u32[]{:S(2)}) collective-permute-start(bf16[2,1,16,512]{3,2,1,0:T(8,128)(2,1)S(1)} %get-tuple-element.56), channel_id=1, source_target_pairs={{0,16},{16,32},{32,48},{48,64},{64,80},{80,96},{96,112},{1,17},{17... | collective-permute-start | bytes 98312 | tf_op jit(solution)/shard_map/ppermute | solution.py:18
  18.0 1.3 collective-permute-start.1
  19.3 0.7 convert_multiply_fusion.4
  20.1 1.0 fusion.43
  21.5 32.6 %all-reduce.6 = (f32[32]{0:T(128)S(1)}, f32[32]{0:T(128)S(1)}) all-reduce(f32[32]{0:T(128)S(1)} %reduce_sum.192, f32[32]{0:T(128)S(1)} %reduce_sum.190), channel_id=1, replica_groups=mesh['pipe'=2,'slab'=8,'dp'=16] {'slab'}, use_global_device_ids=true, to_apply=%region_5.0 | all-reduce | flops 64 | bytes 512 | tf_op jit(solution)/shard_map/psum | solution.py:118
  54.1 0.7 dynamic-slice_bitcast_fusion
  55.9 0.7 add_rsqrt_fusion.1
  57.3 0.7 constant_dynamic-update-slice_fusion.26
  58.0 0.6 constant_dynamic-update-slice_fusion.25
  58.6 0.6 constant_dynamic-update-slice_fusion.24
  59.3 0.6 constant_dynamic-update-slice_fusion.23
  59.9 0.6 constant_dynamic-update-slice_fusion.22
  60.6 0.6 constant_dynamic-update-slice_fusion.21
  61.2 0.6 constant_dynamic-update-slice_fusion.20
  61.9 0.6 constant_dynamic-update-slice_fusion.19
  62.5 0.6 constant_dynamic-update-slice_fusion.18
  63.1 0.6 constant_dynamic-update-slice_fusion.17
  63.8 0.6 constant_dynamic-update-slice_fusion.16
  64.4 0.6 constant_dynamic-update-slice_fusion.15
  65.1 0.6 constant_dynamic-update-slice_fusion.14
  65.7 0.6 constant_dynamic-update-slice_fusion.13
  66.4 0.6 constant_dynamic-update-slice_fusion.12
  67.0 0.6 constant_dynamic-update-slice_fusion.11
  67.7 0.6 constant_dynamic-update-slice_fusion.10
  68.3 0.6 constant_dynamic-update-slice_fusion.9
  68.9 0.6 constant_dynamic-update-slice_fusion.8
  69.6 0.6 constant_dynamic-update-slice_fusion.7
  70.2 0.6 constant_dynamic-update-slice_fusion.6
  70.9 0.6 constant_dynamic-update-slice_fusion.5
  71.5 0.6 constant_dynamic-update-slice_fusion.4
  72.2 0.6 constant_dynamic-update-slice_fusion.3
  72.8 0.6 constant_dynamic-update-slice_fusion.2
  73.4 0.6 constant_dynamic-update-slice_fusion.1
  74.1 0.6 constant_dynamic-update-slice_fusion
  74.7 94.1 %all-gather.5.cloned.1.call-done = bf16[1,512,13824]{2,1,0:T(8,128)(2,1)} async-done(((bf16[1,32,13824]{2,1,0:T(8,128)(2,1)}), bf16[1,512,13824]{2,1,0:T(8,128)(2,1)}) %all-gather.5.cloned.1.call-update) | async-done | bytes 14155792 | tf_op jit(solution)/shard_map/all_gather | solution.py:105
  168.8 18.7 %copy.100 = bf16[1,512,13824]{1,2,0:T(8,128)(2,1)} copy(bf16[1,512,13824]{2,1,0:T(8,128)(2,1)} %all-gather.5.cloned.1.call-done) | data formatting | bytes 28311552 | tf_op jit(solution)/shard_map/all_gather | solution.py:105
  187.5 10.0 %fusion.42 = (f32[512]{0:T(512)S(1)}, f32[512]{0:T(512)S(1)}, f32[512]{0:T(512)S(1)}, f32[512]{0:T(512)S(1)}, f32[2,2,16,512]{3,2,1,0:T(8,128)S(1)}) fusion(f32[512]{0:T(512)S(1)} %sub.59, f32[512]{0:T(512)S(1)} %mul.241, bf16[1,2,1,2,2,16,512]{6,5,4,3,2,1,0:T(8,128)(2,1)S(1)} %copy-done.3, f32[512]{0:T(512)S(1)} %bitcast.571, ...), kind=kOutput, calls=%fused_computation.193 | convolution fusion | flops 906655744 | bytes 16138248 | tf_op jit(solution)/shard_map/tfrwo,oti->frwi/dot_general | solution.py:139
  197.9 31.7 %all-reduce.5 = (f32[32]{0:T(128)S(1)}, f32[32]{0:T(128)S(1)}, f32[32]{0:T(128)S(1)}, f32[32]{0:T(128)S(1)}) all-reduce(f32[32]{0:T(128)S(1)} %reduce_sum.196, f32[32]{0:T(128)S(1)} %reduce_sum.194, f32[32]{0:T(128)S(1)} %reduce_sum.200, f32[32]{0:T(128)S(1)} %reduce_sum.198), channel_id=1, replica_groups=mesh['pipe'=2,'slab'=8,'dp'=16] {'slab'}, use_global_device_ids=true, to_apply=%region_11.12 | all-reduce | flops 128 | bytes 1024 | tf_op jit(solution)/shard_map/psum | solution.py:148
  229.6 0.6 broadcast_divide_fusion.3
  230.7 1.3 collective-permute-start.2
  232.0 1.8 collective-permute-done.2
  233.8 1.3 collective-permute-start.3
  235.1 1.3 collective-permute-start.4
  236.4 0.7 add_rsqrt_fusion
  237.4 8.5 %collective-permute-start.5 = (bf16[2,1,16,512]{3,2,1,0:T(8,128)(2,1)S(1)}, bf16[2,1,16,512]{3,2,1,0:T(8,128)(2,1)S(1)}, u32[]{:S(2)}, u32[]{:S(2)}) collective-permute-start(bf16[2,1,16,512]{3,2,1,0:T(8,128)(2,1)S(1)} %get-tuple-element.52), channel_id=1, source_target_pairs={{0,16},{16,32},{32,48},{48,64},{64,80},{80,96},{96,112},{1,17},{17... | collective-permute-start | bytes 98312 | tf_op jit(solution)/shard_map/ppermute | solution.py:18
  245.9 1.3 collective-permute-start.6
  247.9 9.4 %fusion.6 = f32[2,2,16,512]{3,2,0,1:T(8,128)S(1)} fusion(bf16[512,27,512,1,1]{0,2,3,4,1:T(8,128)(2,1)} %bitcast.561, bf16[27,2,2,16,512]{4,3,2,1,0:T(8,128)(2,1)S(1)} %constant_dynamic-update-slice_fusion.27), kind=kOutput, calls=%fused_computation.63 | convolution fusion | flops 905969664 | bytes 16056320 | tf_op jit(solution)/shard_map/tfrwo,oti->frwi/dot_general | solution.py:139
  257.5 8.7 %collective-permute-start.7 = (bf16[2,1,16,512]{3,2,1,0:T(8,128)(2,1)S(1)}, bf16[2,1,16,512]{3,2,1,0:T(8,128)(2,1)S(1)}, u32[]{:S(2)}, u32[]{:S(2)}) collective-permute-start(bf16[2,1,16,512]{3,2,1,0:T(8,128)(2,1)S(1)} %get-tuple-element.50), channel_id=1, source_target_pairs={{0,16},{16,32},{32,48},{48,64},{64,80},{80,96},{96,112},{1,17},{17... | collective-permute-start | bytes 98312 | tf_op jit(solution)/shard_map/ppermute | solution.py:18
  266.2 1.3 collective-permute-start.8
  267.8 9.0 %collective-permute-done.8 = bf16[2,1,16,512]{3,2,1,0:T(8,128)(2,1)S(1)} collective-permute-done((bf16[2,1,16,512]{3,2,1,0:T(8,128)(2,1)S(1)}, bf16[2,1,16,512]{3,2,1,0:T(8,128)(2,1)S(1)}, u32[]{:S(2)}, u32[]{:S(2)}) %collective-permute-start.8) | collective-permute-done | bytes 32800 | tf_op jit(solution)/shard_map/ppermute | solution.py:19
  278.0 1.7 copy-done.2
  279.7 9.1 %fusion = bf16[512,27,512]{0,2,1:T(8,128)(2,1)} fusion(bf16[27,2,2,2,16,512]{5,4,3,2,1,0:T(8,128)(2,1)} %copy-done.2, bf16[1,2,2,16,512]{4,3,2,1,0:T(8,128)(2,1)S(1)} %bitcast.564, bf16[1,2,2,16,512]{4,3,2,1,0:T(8,128)(2,1)S(1)} %get-tuple-element.46), kind=kOutput, calls=%fused_computation.1 | convolution fusion | flops 1826160640 | bytes 17825792 | tf_op jit(solution)/shard_map/kfrwo,tkfrwi->oti/dot_general | solution.py:170
  288.8 18.6 %copy.107 = bf16[512,13824]{1,0:T(8,128)(2,1)} copy(bf16[512,13824]{0,1:T(8,128)(2,1)} %bitcast.562) | data formatting | bytes 28311552 | tf_op jit(solution)/shard_map/convert_element_type | solution.py:174
  307.5 193.0 %reduce-scatter.2.cloned.1.call-done = bf16[32,13824]{1,0:T(8,128)(2,1)} async-done(((bf16[512,13824]{1,0:T(8,128)(2,1)}), bf16[32,13824]{1,0:T(8,128)(2,1)}) %reduce-scatter.2.cloned.1.call-update) | async-done | bytes 884752 | tf_op jit(solution)/shard_map/reduce_scatter | solution.py:173
  500.5 2.5 all_gather.16
  503.5 35.2 %all-reduce.4 = (f32[32]{0:T(128)S(1)}, f32[32]{0:T(128)S(1)}, f32[1,512]{1,0:T(1,128)S(1)}, f32[1,512]{1,0:T(1,128)S(1)}, f32[1,512]{1,0:T(1,128)S(1)}, /*index=5*/f32[1,512]{1,0:T(1,128)S(1)}) all-reduce(f32[32]{0:T(128)S(1)} %reduce_sum.204, f32[32]{0:T(128)S(1)} %reduce_sum.202, ...), channel_id=1, replica_groups=mesh['pipe'=2,'slab'=8,'dp'=16] {'slab'}, use_global_device_ids=true, to_apply=%region_23.24 | all-reduce | flops 2112 | bytes 16896 | tf_op jit(solution)/shard_map/psum | solution.py:148
  538.7 0.6 broadcast_in_dim.47
  539.3 0.6 broadcast_divide_fusion.1
  540.1 0.7 broadcast_divide_fusion
  541.0 0.7 maximum_bitcast_fusion
  541.7 229.5 %all-gather.7.cloned.1.call-done = f32[256,13824]{1,0:T(8,128)} async-done(((f32[32,13824]{1,0:T(8,128)}), f32[256,13824]{1,0:T(8,128)}) %all-gather.7.cloned.1.call-update) | async-done | bytes 14155792 | tf_op jit(solution)/shard_map/all_gather | solution.py:181
  771.2 7.3 reduce_sum.205
  (131 shorter events, 6.2 us)
Async XLA Ops:
  7.2 48.2 %copy-start = (bf16[1,1000,1024]{2,1,0:T(8,128)(2,1)S(1)}, bf16[1,1000,1024]{2,1,0:T(8,128)(2,1)}, u32[]{:S(2)}) copy-start(bf16[1,1000,1024]{2,1,0:T(8,128)(2,1)} %param.11) | copy-start | bytes 6144004
  7.2 161.6 %all-gather.5.cloned.1.call-start = ((), (), s32[]{:S(2)}) async-start(), calls=%async_computation.2 | async-start | bytes 15040512 | tf_op jit(solution)/shard_map/all_gather | solution.py:105
  7.9 492.6 %reduce-scatter.2.cloned.1.call-start = ((), (), s32[]{:S(2)}) async-start(), calls=%async_computation.1 | async-start | bytes 15040512 | tf_op jit(solution)/shard_map/reduce_scatter | solution.py:173
  8.9 48.4 %collective-permute-start = (bf16[2,1,16,512]{3,2,1,0:T(8,128)(2,1)S(1)}, bf16[2,1,16,512]{3,2,1,0:T(8,128)(2,1)S(1)}, u32[]{:S(2)}, u32[]{:S(2)}) collective-permute-start(bf16[2,1,16,512]{3,2,1,0:T(8,128)(2,1)S(1)} %get-tuple-element.56), channel_id=1, source_target_pairs={{0,16},{16,32},{32,48},{48,64},{64,80},{80,96},{96,112},{1,17},{17... | collective-permute-start | bytes 98312 | tf_op jit(solution)/shard_map/ppermute | solution.py:18
  18.0 39.3 %collective-permute-start.1 = (bf16[2,1,16,512]{3,2,1,0:T(8,128)(2,1)S(1)}, bf16[2,1,16,512]{3,2,1,0:T(8,128)(2,1)S(1)}, u32[]{:S(2)}, u32[]{:S(2)}) collective-permute-start(bf16[2,1,16,512]{3,2,1,0:T(8,128)(2,1)S(1)} %get-tuple-element.57), channel_id=1, source_target_pairs={{16,0},{32,16},{48,32},{64,48},{80,64},{96,80},{112,96},{17,1},{33... | collective-permute-start | bytes 98312 | tf_op jit(solution)/shard_map/ppermute | solution.py:19
  55.4 10.3 %copy-start.4 = (bf16[2,1,2,2,16,512]{5,4,3,2,1,0:T(8,128)(2,1)S(1)}, bf16[2,1,2,2,16,512]{5,4,3,2,1,0:T(8,128)(2,1)}, u32[]{:S(2)}) copy-start(bf16[2,1,2,2,16,512]{5,4,3,2,1,0:T(8,128)(2,1)} %param.8) | copy-start | bytes 393220
  55.4 10.3 %copy-start.5 = (bf16[1,2,2,16,512]{4,3,2,1,0:T(8,128)(2,1)S(1)}, bf16[1,2,2,16,512]{4,3,2,1,0:T(8,128)(2,1)}, u32[]{:S(2)}) copy-start(bf16[1,2,2,16,512]{4,3,2,1,0:T(8,128)(2,1)} %param.9) | copy-start | bytes 196612
  74.7 112.8 %copy-start.3 = (bf16[1,2,1,2,2,16,512]{6,5,4,3,2,1,0:T(8,128)(2,1)S(1)}, bf16[1,2,1,2,2,16,512]{6,5,4,3,2,1,0:T(8,128)(2,1)}, u32[]{:S(2)}) copy-start(bf16[1,2,1,2,2,16,512]{6,5,4,3,2,1,0:T(8,128)(2,1)} %param.7) | copy-start | bytes 393220
  230.7 3.1 collective-permute-start.2
  233.8 13.3 %collective-permute-start.3 = (bf16[2,1,16,512]{3,2,1,0:T(8,128)(2,1)S(1)}, bf16[2,1,16,512]{3,2,1,0:T(8,128)(2,1)S(1)}, u32[]{:S(2)}, u32[]{:S(2)}) collective-permute-start(bf16[2,1,16,512]{3,2,1,0:T(8,128)(2,1)S(1)} %get-tuple-element.54), channel_id=1, source_target_pairs={{0,16},{16,32},{32,48},{48,64},{64,80},{80,96},{96,112},{1,17},{17... | collective-permute-start | bytes 98312 | tf_op jit(solution)/shard_map/ppermute | solution.py:18
  235.1 12.0 %collective-permute-start.4 = (bf16[2,1,16,512]{3,2,1,0:T(8,128)(2,1)S(1)}, bf16[2,1,16,512]{3,2,1,0:T(8,128)(2,1)S(1)}, u32[]{:S(2)}, u32[]{:S(2)}) collective-permute-start(bf16[2,1,16,512]{3,2,1,0:T(8,128)(2,1)S(1)} %get-tuple-element.55), channel_id=1, source_target_pairs={{16,0},{32,16},{48,32},{64,48},{80,64},{96,80},{112,96},{17,1},{33... | collective-permute-start | bytes 98312 | tf_op jit(solution)/shard_map/ppermute | solution.py:19
  237.4 30.1 %collective-permute-start.5 = (bf16[2,1,16,512]{3,2,1,0:T(8,128)(2,1)S(1)}, bf16[2,1,16,512]{3,2,1,0:T(8,128)(2,1)S(1)}, u32[]{:S(2)}, u32[]{:S(2)}) collective-permute-start(bf16[2,1,16,512]{3,2,1,0:T(8,128)(2,1)S(1)} %get-tuple-element.52), channel_id=1, source_target_pairs={{0,16},{16,32},{32,48},{48,64},{64,80},{80,96},{96,112},{1,17},{17... | collective-permute-start | bytes 98312 | tf_op jit(solution)/shard_map/ppermute | solution.py:18
  245.9 21.6 %collective-permute-start.6 = (bf16[2,1,16,512]{3,2,1,0:T(8,128)(2,1)S(1)}, bf16[2,1,16,512]{3,2,1,0:T(8,128)(2,1)S(1)}, u32[]{:S(2)}, u32[]{:S(2)}) collective-permute-start(bf16[2,1,16,512]{3,2,1,0:T(8,128)(2,1)S(1)} %get-tuple-element.53), channel_id=1, source_target_pairs={{16,0},{32,16},{48,32},{64,48},{80,64},{96,80},{112,96},{17,1},{33... | collective-permute-start | bytes 98312 | tf_op jit(solution)/shard_map/ppermute | solution.py:19
  257.5 10.3 %collective-permute-start.7 = (bf16[2,1,16,512]{3,2,1,0:T(8,128)(2,1)S(1)}, bf16[2,1,16,512]{3,2,1,0:T(8,128)(2,1)S(1)}, u32[]{:S(2)}, u32[]{:S(2)}) collective-permute-start(bf16[2,1,16,512]{3,2,1,0:T(8,128)(2,1)S(1)} %get-tuple-element.50), channel_id=1, source_target_pairs={{0,16},{16,32},{32,48},{48,64},{64,80},{80,96},{96,112},{1,17},{17... | collective-permute-start | bytes 98312 | tf_op jit(solution)/shard_map/ppermute | solution.py:18
  266.2 10.6 %collective-permute-start.8 = (bf16[2,1,16,512]{3,2,1,0:T(8,128)(2,1)S(1)}, bf16[2,1,16,512]{3,2,1,0:T(8,128)(2,1)S(1)}, u32[]{:S(2)}, u32[]{:S(2)}) collective-permute-start(bf16[2,1,16,512]{3,2,1,0:T(8,128)(2,1)S(1)} %get-tuple-element.51), channel_id=1, source_target_pairs={{16,0},{32,16},{48,32},{64,48},{80,64},{96,80},{112,96},{17,1},{33... | collective-permute-start | bytes 98312 | tf_op jit(solution)/shard_map/ppermute | solution.py:19
  278.0 1.7 copy-start.2
  307.5 463.7 %all-gather.7.cloned.1.call-start = ((), (), s32[]{:S(2)}) async-start(), calls=%async_computation.3 | async-start | bytes 15925248 | tf_op jit(solution)/shard_map/all_gather | solution.py:181
  771.2 7.3 copy-start.1
Sparse Core Ops, SparseCore 0:
  9.8 158.9 all-gather.4
  307.6 192.8 reduce-scatter.1
  503.7 267.3 all-gather.6
